TPU v7x, 32 devices: a whole 2x2x4 slice. The times are simulated.
32 devices in a mesh: leaf: 16 (over z, y, x), col: 2 (over core).
Axes of the slice: x: 2, y: 2, z: 4, core: 2. Of those that a mesh axis runs over, the one named last changes fastest.
Arguments:
- sources: bfloat16 [65536, 256], P('leaf', 'col'), may hold values from -6 to 6
- near_tiles: bfloat16 [256, 8, 256, 256], P('leaf', 'col'), may hold values from -0.125 to 0.125
- near_index: int32 [256, 8], P('leaf'), may hold values from 0 to 255, as said below
- near_count: int32 [256], P('leaf'), may hold values from 1 to 8, as said below
- leaf_basis: bfloat16 [256, 64, 256], P('leaf'), may hold values from -0.375 to 0.375
- leaf_coupling: bfloat16 [256, 64, 256], P('leaf'), may hold values from -0.375 to 0.375
- leaf_far: int32 [256, 4], P('leaf'), may hold values from 0 to 255, as said below
- up_leaf: bfloat16 [32, 64, 512], P('leaf'), may hold values from -0.25 to 0.25
- mid_coupling: bfloat16 [32, 64, 256], P('leaf'), may hold values from -0.375 to 0.375
- mid_far: int32 [32, 4], P('leaf'), may hold values from 0 to 31, as said below
- up_mid: bfloat16 [32, 64, 64], P('leaf'), may hold values from -0.75 to 0.75
- top_coupling: bfloat16 [4, 64, 256], replicated, may hold values from -0.4375 to 0.4375
Outputs:
- product: float32 [65536, 256], P('leaf', 'col')
Inputs may be any that keep to these rules, and one draw needn't show every extreme that they name: `near_index`: entry 0 of row i is i; the other 7 entries are distinct leaves j with j != i and |i - j| <= 8. Only the first near_count[i] slots of leaf i count; some leaf has all 8. `leaf_far`: row i holds 4 distinct leaves j != i with |i // 8 - j // 8| <= 1. `mid_far`: row a holds 4 distinct middle clusters b != a with |a // 8 - b // 8| <= 1.
All inputs are finite; a program needn't handle non-finite values.
Results may differ from a plain program's by a relative error of at most 0.01.
Values may be sent and summed in bfloat16 or wider, within the bound.
No kernel may reach another device: no remote copies, remote signals or barrier semaphores. Data moves between devices by JAX's collectives and lax.ppermute only.
A program may use at most 128 MiB of HBM per device.

v0:
```python
import jax
import jax.numpy as jnp
from jax import lax
from jax.sharding import PartitionSpec as P

CHILD = 8
FAR = 4


def padded(x, sides, width):
    for axis, dim in sides:
        size, length = (lax.axis_size(axis), x.shape[dim])
        up = [(i, (i + 1) % size) for i in range(size - 1)]
        down = [(j, i) for i, j in up]
        last = lax.slice_in_dim(x, length - width, length, axis=dim)
        first = lax.slice_in_dim(x, 0, width, axis=dim)
        before = lax.ppermute(last, axis, up)
        after = lax.ppermute(first, axis, down)
        x = jnp.concatenate([before, x, after], axis=dim)
    return x


def shards(
    sources,
    near_tiles,
    near_index,
    near_count,
    leaf_basis,
    leaf_coupling,
    leaf_far,
    up_leaf,
    mid_coupling,
    mid_far,
    up_mid,
    top_coupling,
):
    f32 = jnp.float32
    bf16 = jnp.bfloat16
    leaf_count = leaf_basis.shape[0]
    rank_size = leaf_basis.shape[1]
    leaf_size = leaf_basis.shape[2]
    col_count = sources.shape[1]
    mid_count = leaf_count // CHILD
    total_top = top_coupling.shape[0]
    device = lax.axis_index("leaf")
    first_leaf = device * leaf_count
    first_mid = device * mid_count
    window = padded(sources, (("leaf", 0),), CHILD * leaf_size)
    near_local = near_index - (first_leaf - CHILD)
    all_tiles = lax.all_gather(near_tiles, "col", axis=1, tiled=True)
    slot_count = all_tiles.shape[1]
    blocks = window.reshape(-1, leaf_size, window.shape[1])
    picked = blocks[near_local]
    live_mask = jnp.arange(slot_count)[None, :] < near_count[:, None]
    picked = jnp.where(live_mask[:, :, None, None], picked, jnp.zeros((), bf16))
    result = jnp.einsum("lsij,lsjc->lic", all_tiles, picked, preferred_element_type=f32)
    near_part = result.reshape(leaf_count * leaf_size, window.shape[1])
    leaf_blocks = sources.reshape(leaf_count, leaf_size, col_count)
    leaf_coef = jnp.einsum(
        "lrk,lkc->lrc", leaf_basis, leaf_blocks, preferred_element_type=f32
    ).astype(bf16)
    mid_coef = jnp.einsum(
        "qrk,qkc->qrc",
        up_leaf,
        leaf_coef.reshape(mid_count, CHILD * rank_size, col_count),
        preferred_element_type=f32,
    ).astype(bf16)
    mid_lift = jnp.einsum("qrs,qsc->qrc", up_mid, mid_coef, preferred_element_type=f32).astype(bf16)
    parent = (first_mid + jnp.arange(mid_count)) // CHILD
    mid_flat = mid_far.reshape(-1)
    top_range = jnp.arange(total_top)
    coef_piece = lax.all_gather(mid_coef, "leaf", axis=0, tiled=True)
    lift_piece = lax.all_gather(mid_lift, "leaf", axis=0, tiled=True)
    global_ids = jnp.arange(coef_piece.shape[0])
    group_map = (top_range[:, None] == (global_ids // CHILD)[None, :]).astype(bf16)
    top_total = jnp.einsum("pk,krc->prc", group_map, lift_piece, preferred_element_type=f32)
    global_ids = jnp.arange(coef_piece.shape[0])
    pick_map = (mid_flat[:, None] == global_ids[None, :]).astype(bf16)
    mid_picked = jnp.einsum("ik,krc->irc", pick_map, coef_piece, preferred_element_type=f32)
    top_coef = top_total.astype(bf16)
    parent_rows = top_coupling[parent]
    keep_mask = top_range[None, :] != parent[:, None]
    stacked = jnp.where(keep_mask[:, :, None, None], top_coef[None], jnp.zeros((), bf16))
    top_field = jnp.einsum(
        "qrk,qkc->qrc",
        parent_rows,
        stacked.reshape(mid_count, total_top * rank_size, col_count),
        preferred_element_type=f32,
    ).astype(bf16)
    mid_chosen = mid_picked.astype(bf16).reshape(mid_count, FAR * rank_size, col_count)
    mid_field = (
        jnp.einsum("qrk,qkc->qrc", mid_coupling, mid_chosen, preferred_element_type=f32)
        + jnp.einsum("qrs,qrc->qsc", up_mid, top_field, preferred_element_type=f32)
    ).astype(bf16)
    leaf_window = padded(leaf_coef, (("leaf", 0),), CHILD)
    far_local = leaf_far - (first_leaf - CHILD)
    leaf_chosen = leaf_window[far_local].reshape(leaf_count, FAR * rank_size, col_count)
    down_part = jnp.einsum("qrs,qrc->qsc", up_leaf, mid_field, preferred_element_type=f32).reshape(
        leaf_count, rank_size, col_count
    )
    leaf_field = (
        jnp.einsum("lrk,lkc->lrc", leaf_coupling, leaf_chosen, preferred_element_type=f32)
        + down_part
    ).astype(bf16)
    far_part = jnp.einsum(
        "lrk,lrc->lkc", leaf_basis, leaf_field, preferred_element_type=f32
    ).reshape(leaf_count * leaf_size, col_count)
    return near_part + far_part


def solution(mesh):
    return jax.shard_map(
        shards,
        mesh=mesh,
        in_specs=(
            P("leaf", "col"),
            P("leaf", "col", None, None),
            P("leaf", None),
            P("leaf"),
            P("leaf", None, None),
            P("leaf", None, None),
            P("leaf", None),
            P("leaf", None, None),
            P("leaf", None, None),
            P("leaf", None),
            P("leaf", None, None),
            P(),
        ),
        out_specs=P("leaf", "col"),
        check_vma=False,
    )
```

profile of v0, /device:TPU:0, one launch (start us, length us, event | category | flops | bytes accessed | tf_op | source)
XLA Modules:
  0.0 168.7 jit_solution(13844385451105794318)
XLA Ops:
  6.5 0.7 all-gather.2.cloned.1.call-update
  7.3 0.2 copy-done
  7.6 0.3 copy-done.1
  7.9 0.3 convolution_convert_fusion
  8.3 4.9 %collective-permute-start.2 = (bf16[8,64,128]{2,1,0:T(8,128)(2,1)S(1)}, bf16[8,64,128]{2,1,0:T(8,128)(2,1)S(1)}, u32[]{:S(2)}, u32[]{:S(2)}) collective-permute-start(bf16[8,64,128]{2,1,0:T(8,128)(2,1)S(1)} %get-tuple-element.7), channel_id=1, source_target_pairs={{0,2},{2,4},{4,6},{6,8},{8,10},{10,12},{12,14},{14,16},{16,18},{18... | collective-permute-start | bytes 393224 | tf_op jit(solution)/shard_map/ppermute | solution.py:17
  13.2 1.3 collective-permute-start.3
  14.5 1.1 fusion.33
  15.5 5.4 %collective-permute-start = (bf16[2048,128]{1,0:T(8,128)(2,1)}, bf16[2048,128]{1,0:T(8,128)(2,1)}, u32[]{:S(2)}, u32[]{:S(2)}) collective-permute-start(bf16[2048,128]{1,0:T(8,128)(2,1)} %get-tuple-element.5), channel_id=1, source_target_pairs={{0,2},{2,4},{4,6},{6,8},{8,10},{10,12},{12,14},{14,16},{16,18},{18... | collective-permute-start | bytes 1572872 | tf_op jit(solution)/shard_map/ppermute | solution.py:17
  20.9 1.3 collective-permute-start.1
  22.7 57.8 %all_gather.11 = bf16[32,64,128]{2,1,0:T(8,128)(2,1)S(1)} all-gather(bf16[2,64,128]{2,1,0:T(8,128)(2,1)S(1)} %fusion.12), channel_id=1, replica_groups=mesh['leaf'=16,'col'=2] {'leaf'}, dimensions={0}, use_global_device_ids=true | all-gather | bytes 557056 | tf_op jit(solution)/shard_map/all_gather | solution.py:73
  80.5 0.4 convolution_convert_fusion.2
  81.3 38.7 %all_gather.10 = bf16[32,64,128]{2,1,0:T(8,128)(2,1)S(1)} all-gather(bf16[2,64,128]{2,1,0:T(8,128)(2,1)S(1)} %bitcast.59), channel_id=1, replica_groups=mesh['leaf'=16,'col'=2] {'leaf'}, dimensions={0}, use_global_device_ids=true | all-gather | bytes 557056 | tf_op jit(solution)/shard_map/all_gather | solution.py:72
  119.9 0.4 convolution_convert_fusion.1
  120.4 0.6 gather_fusion.2
  121.1 0.4 fusion.11
  121.5 0.4 convolution_bitcast_fusion.1
  122.3 1.0 pad_maximum_fusion.1
  123.3 0.7 gather_fusion.1
  124.0 1.9 %fusion.9 = f32[16,128,256]{2,1,0:T(8,128)} fusion(bf16[16,64,256]{2,1,0:T(8,128)(2,1)S(1)} %copy-done, f32[16,64,128]{2,1,0:T(8,128)S(1)} %bitcast.57, bf16[16,64,256]{2,1,0:T(8,128)(2,1)S(1)} %copy-done.3, bf16[16,256,128]{2,1,0:T(8,128)(2,1)S(1)} %bitcast.56), kind=kOutput, calls=%fused_computation.15 | convolution fusion | flops 134479872 | bytes 4718592 | tf_op jit(solution)/shard_map/lrk,lrc->lkc/dot_general | solution.py:105
  126.0 1.7 pad_maximum_fusion
  127.6 6.6 %gather_fusion = bf16[128,256,128]{2,1,0:T(8,128)(2,1)} fusion(bf16[32,256,128]{2,1,0:T(8,128)(2,1)S(1)} %bitcast.52, s32[1024]{0:T(1024)S(1)} %pad_clamp_fusion.2), kind=kCustom, calls=%fused_computation | custom fusion | bytes 16777728 | tf_op jit(solution)/shard_map/gather | solution.py:53
  134.2 12.1 %copy.26 = bf16[128,256,128]{1,2,0:T(8,128)(2,1)} copy(bf16[128,256,128]{2,1,0:T(8,128)(2,1)} %gather_fusion) | data formatting | bytes 16777216 | tf_op jit(solution)/shard_map/gather | solution.py:53
  146.3 12.7 %fusion.4 = f32[16,256,128]{1,2,0:T(8,128)} fusion(f32[16,128,256]{2,1,0:T(8,128)S(1)} %copy-done.2, bf16[16,8,256,256]{3,2,1,0:T(8,128)(2,1)} %all-gather.2.cloned.1.call-done, bf16[16,8,256,128]{2,3,1,0:T(8,128)(2,1)} %bitcast.54, pred[16,8]{1,0:T(8,128)(4,1)S(1)} %iota_compare_fusion), kind=kOutput, calls=%fused_computation.9 | convolution fusion | flops 2152202240 | bytes 29360256 | tf_op jit(solution)/shard_map/lsij,lsjc->lic/dot_general | solution.py:56
  159.0 2.9 %copy.34 = f32[16,256,128]{2,1,0:T(8,128)} copy(f32[16,256,128]{1,2,0:T(8,128)} %fusion.4) | data formatting | bytes 4194304 | tf_op jit(solution)/shard_map/add | solution.py:108
  (51 shorter events, 1.4 us)
Async XLA Ops:
  6.5 1.0 copy-start
  6.5 1.4 copy-start.1
  6.5 139.8 %all-gather.2.cloned.1.call-start = ((), (), s32[]{:S(2)}) async-start(), calls=%async_computation | async-start | bytes 25165824 | tf_op jit(solution)/shard_map/all_gather | solution.py:50
  7.3 14.9 %copy-start.9 = (s32[16,4]{0,1:T(4,128)S(1)}, s32[16,4]{0,1:T(4,128)}, u32[]{:S(2)}) copy-start(s32[16,4]{0,1:T(4,128)} %param.18) | copy-start | bytes 772
  7.3 15.1 %copy-start.4 = (bf16[2,64,512]{2,1,0:T(8,128)(2,1)S(1)}, bf16[2,64,512]{2,1,0:T(8,128)(2,1)}, u32[]{:S(2)}) copy-start(bf16[2,64,512]{2,1,0:T(8,128)(2,1)} %param.19) | copy-start | bytes 393220
  7.3 15.3 %copy-start.6 = (bf16[2,64,64]{2,1,0:T(8,128)(2,1)S(1)}, bf16[2,64,64]{2,1,0:T(8,128)(2,1)}, u32[]{:S(2)}) copy-start(bf16[2,64,64]{2,1,0:T(8,128)(2,1)} %param.22) | copy-start | bytes 49156
  7.3 73.9 %copy-start.11 = (s32[2,4]{1,0:T(2,128)S(1)}, s32[2,4]{1,0:T(2,128)}, u32[]{:S(2)}) copy-start(s32[2,4]{1,0:T(2,128)} %param.21) | copy-start | bytes 100
  7.3 113.1 %copy-start.7 = (bf16[4,64,256]{2,1,0:T(8,128)(2,1)S(1)}, bf16[4,64,256]{2,1,0:T(8,128)(2,1)}, u32[]{:S(2)}) copy-start(bf16[4,64,256]{2,1,0:T(8,128)(2,1)} %param.23) | copy-start | bytes 393220
  7.3 113.7 %copy-start.10 = (s32[16]{0:T(128)S(1)}, s32[16]{0:T(128)}, u32[]{:S(2)}) copy-start(s32[16]{0:T(128)} %param.15) | copy-start | bytes 196
  7.3 113.7 %copy-start.8 = (s32[16,8]{0,1:T(8,128)S(1)}, s32[16,8]{0,1:T(8,128)}, u32[]{:S(2)}) copy-start(s32[16,8]{0,1:T(8,128)} %param.14) | copy-start | bytes 1540
  7.3 114.1 %copy-start.5 = (bf16[2,64,256]{2,1,0:T(8,128)(2,1)S(1)}, bf16[2,64,256]{2,1,0:T(8,128)(2,1)}, u32[]{:S(2)}) copy-start(bf16[2,64,256]{2,1,0:T(8,128)(2,1)} %param.20) | copy-start | bytes 196612
  8.3 114.0 %collective-permute-start.2 = (bf16[8,64,128]{2,1,0:T(8,128)(2,1)S(1)}, bf16[8,64,128]{2,1,0:T(8,128)(2,1)S(1)}, u32[]{:S(2)}, u32[]{:S(2)}) collective-permute-start(bf16[8,64,128]{2,1,0:T(8,128)(2,1)S(1)} %get-tuple-element.7), channel_id=1, source_target_pairs={{0,2},{2,4},{4,6},{6,8},{8,10},{10,12},{12,14},{14,16},{16,18},{18... | collective-permute-start | bytes 393224 | tf_op jit(solution)/shard_map/ppermute | solution.py:17
  13.2 109.1 %collective-permute-start.3 = (bf16[8,64,128]{2,1,0:T(8,128)(2,1)S(1)}, bf16[8,64,128]{2,1,0:T(8,128)(2,1)}, u32[]{:S(2)}, u32[]{:S(2)}) collective-permute-start(bf16[8,64,128]{2,1,0:T(8,128)(2,1)S(1)} %get-tuple-element.8), channel_id=1, source_target_pairs={{2,0},{4,2},{6,4},{8,6},{10,8},{12,10},{14,12},{16,14},{18,16},{20... | collective-permute-start | bytes 393224 | tf_op jit(solution)/shard_map/ppermute | solution.py:18
  15.5 110.4 %collective-permute-start = (bf16[2048,128]{1,0:T(8,128)(2,1)}, bf16[2048,128]{1,0:T(8,128)(2,1)}, u32[]{:S(2)}, u32[]{:S(2)}) collective-permute-start(bf16[2048,128]{1,0:T(8,128)(2,1)} %get-tuple-element.5), channel_id=1, source_target_pairs={{0,2},{2,4},{4,6},{6,8},{8,10},{10,12},{12,14},{14,16},{16,18},{18... | collective-permute-start | bytes 1572872 | tf_op jit(solution)/shard_map/ppermute | solution.py:17
  20.9 105.1 %collective-permute-start.1 = (bf16[2048,128]{1,0:T(8,128)(2,1)}, bf16[2048,128]{1,0:T(8,128)(2,1)}, u32[]{:S(2)}, u32[]{:S(2)}) collective-permute-start(bf16[2048,128]{1,0:T(8,128)(2,1)} %get-tuple-element.6), channel_id=1, source_target_pairs={{2,0},{4,2},{6,4},{8,6},{10,8},{12,10},{14,12},{16,14},{18,16},{20... | collective-permute-start | bytes 1572872 | tf_op jit(solution)/shard_map/ppermute | solution.py:18
  22.7 101.3 %copy-start.3 = (bf16[16,64,256]{2,1,0:T(8,128)(2,1)S(1)}, bf16[16,64,256]{2,1,0:T(8,128)(2,1)}, u32[]{:S(2)}) copy-start(bf16[16,64,256]{2,1,0:T(8,128)(2,1)} %param.17) | copy-start | bytes 1572868
  134.2 12.1 %copy-start.2 = (f32[16,128,256]{2,1,0:T(8,128)S(1)}, f32[16,128,256]{2,1,0:T(8,128)}, u32[]{:S(2)}) copy-start(f32[16,128,256]{2,1,0:T(8,128)} %fusion.9) | copy-start | bytes 6291460
Sparse Core Ops, SparseCore 0:
  8.9 32.7 all-gather.1
where the time goes:
time: 169 us
  blocking collectives  96.5 us (57%)
  local copies, waits for them, and re-layouts  25.4 us (15%)
  matrix products  16.8 us (10%)
  between operations  13.7 us (8%)
  starting transfers between devices  12.8 us (8%)
  other arithmetic  2.82 us (2%)
    all_gather x1, blocking collectives, shards(): lift_piece = lax.all_gather(mid_lift, 'leaf', axis=0, tiled=True)  57.8 us
    all_gather x1, blocking collectives, shards(): coef_piece = lax.all_gather(mid_coef, 'leaf', axis=0, tiled=True)  38.7 us
    gather x2, local copies, waits for them, and re-layouts, shards(): picked = blocks[near_local]  18.7 us
    dot_general x1, matrix products, shards(): jnp.einsum('lsij,lsjc->lic', all_tiles, picked, preferred_element_type=f32)  12.7 us
    ppermute x2, starting transfers between devices, padded(): before = lax.ppermute(last, axis, up)  10.2 us
  transfers between devices with their start and end apart: 5, of which 0 were waited for; matrix products, arithmetic and copies ran while one was open for 17% of the time, Pallas kernels for 0%

commit v1 on v0

--- a/solution.py
+++ b/solution.py
@@ -5,6 +5,19 @@
 
 CHILD = 8
 FAR = 4
+
+
+def ring_gather(array, axis, dim):
+    ways = lax.axis_size(axis)
+    up = [(d, (d + 1) % ways) for d in range(ways)]
+    down = [(d, (d - 1) % ways) for d in range(ways)]
+    earlier, later = ([array], [array])
+    for _ in range(ways // 2):
+        earlier.append(lax.ppermute(earlier[-1], axis, up))
+    for _ in range((ways - 1) // 2):
+        later.append(lax.ppermute(later[-1], axis, down))
+    line = jnp.concatenate([*earlier[::-1], *later[1:]], axis=dim)
+    return jnp.roll(line, (lax.axis_index(axis) - ways // 2) * array.shape[dim], axis=dim)
 
 
 def padded(x, sides, width):
@@ -69,7 +82,7 @@
     parent = (first_mid + jnp.arange(mid_count)) // CHILD
     mid_flat = mid_far.reshape(-1)
     top_range = jnp.arange(total_top)
-    coef_piece = lax.all_gather(mid_coef, "leaf", axis=0, tiled=True)
+    coef_piece = ring_gather(mid_coef, "leaf", 0)
     lift_piece = lax.all_gather(mid_lift, "leaf", axis=0, tiled=True)
     global_ids = jnp.arange(coef_piece.shape[0])
     group_map = (top_range[:, None] == (global_ids // CHILD)[None, :]).astype(bf16)

time: 169 us -> 175 us (1.036)
  blocking collectives: 96.5 us -> 46.5 us
  starting transfers between devices: 12.8 us -> 51.2 us
  waiting for transfers between devices: 0.72 us -> 16.4 us
    ppermute x0 -> x15, starting transfers between devices: none -> 42 us  [the longest x7 36.8 us: ring_gather(): later.append(lax.ppermute(later[-1], axis, down))]
    all_gather x1 -> x0, blocking collectives: 38.7 us -> none  [shards(): coef_piece = lax.all_gather(mid_coef, 'leaf', axis=0, tiled=True)]
    ppermute x0 -> x15, waiting for transfers between devices: none -> 15.7 us  [the longest x8 11.2 us: ring_gather(): earlier.append(lax.ppermute(earlier[-1], axis, up))]
    all_gather x1, blocking collectives: 57.8 us -> 46.5 us  [shards(): lift_piece = lax.all_gather(mid_lift, 'leaf', axis=0, tiled=True)]
    ppermute x2, starting transfers between devices: 10.2 us -> 6.63 us  [padded(): before = lax.ppermute(last, axis, up)]
  transfers between devices with their start and end apart: 5 -> 20, of which waited for: 0 -> 7; matrix products, arithmetic and copies ran while one was open for 17% -> 17% of each run, Pallas kernels for 0% -> 0%
where the time goes in v1:
time: 175 us; the launch traced here: 174 us
  starting transfers between devices  51.2 us (29%)
  blocking collectives  46.5 us (27%)
  local copies, waits for them, and re-layouts  25.8 us (15%)
  matrix products  18.3 us (10%)
  waiting for transfers between devices  16.4 us (9%)
  between operations  13.8 us (8%)
  other arithmetic  1.92 us (1%)
    all_gather x1, blocking collectives, shards(): lift_piece = lax.all_gather(mid_lift, 'leaf', axis=0, tiled=True)  46.5 us
    ppermute x7, starting transfers between devices, ring_gather(): later.append(lax.ppermute(later[-1], axis, down))  36.8 us
    gather x2, local copies, waits for them, and re-layouts, shards(): picked = blocks[near_local]  18.7 us
    dot_general x1, matrix products, shards(): jnp.einsum('lsij,lsjc->lic', all_tiles, picked, preferred_element_type=f32)  12.7 us
    ppermute x8, waiting for transfers between devices, ring_gather(): earlier.append(lax.ppermute(earlier[-1], axis, up))  11.2 us
    ppermute x2, starting transfers between devices, padded(): before = lax.ppermute(last, axis, up)  6.63 us
    ppermute x8, starting transfers between devices, ring_gather(): earlier.append(lax.ppermute(earlier[-1], axis, up))  5.25 us
    ppermute x7, waiting for transfers between devices, ring_gather(): later.append(lax.ppermute(later[-1], axis, down))  4.48 us
  transfers between devices with their start and end apart: 20, of which 7 were waited for; matrix products, arithmetic and copies ran while one was open for 17% of the time, Pallas kernels for 0%

profile of v1, /device:TPU:0, one launch (start us, length us, event | category | flops | bytes accessed | tf_op | source)
XLA Modules:
  0.0 174.0 jit_solution(17137755611104302989)
XLA Ops:
  8.4 3.0 %collective-permute-start.4 = (bf16[2,64,128]{2,1,0:T(8,128)(2,1)S(1)}, bf16[2,64,128]{2,1,0:T(8,128)(2,1)S(1)}, u32[]{:S(2)}, u32[]{:S(2)}) collective-permute-start(bf16[2,64,128]{2,1,0:T(8,128)(2,1)S(1)} %bitcast.61), channel_id=1, source_target_pairs={{0,2},{2,4},{4,6},{6,8},{8,10},{10,12},{12,14},{14,16},{16,18},{18... | collective-permute-start | bytes 98312 | tf_op jit(solution)/shard_map/ppermute | solution.py:16
  11.5 4.1 %collective-permute-start.12 = (bf16[2,64,128]{2,1,0:T(8,128)(2,1)S(1)}, bf16[2,64,128]{2,1,0:T(8,128)(2,1)S(1)}, u32[]{:S(2)}, u32[]{:S(2)}) collective-permute-start(bf16[2,64,128]{2,1,0:T(8,128)(2,1)S(1)} %bitcast.62), channel_id=1, source_target_pairs={{0,30},{2,0},{4,2},{6,4},{8,6},{10,8},{12,10},{14,12},{16,14},{18,... | collective-permute-start | bytes 98312 | tf_op jit(solution)/shard_map/ppermute | solution.py:18
  19.2 5.3 %collective-permute-start = (bf16[2048,128]{1,0:T(8,128)(2,1)}, bf16[2048,128]{1,0:T(8,128)(2,1)}, u32[]{:S(2)}, u32[]{:S(2)}) collective-permute-start(bf16[2048,128]{1,0:T(8,128)(2,1)} %get-tuple-element.5), channel_id=1, source_target_pairs={{0,2},{2,4},{4,6},{6,8},{8,10},{10,12},{12,14},{14,16},{16,18},{18... | collective-permute-start | bytes 1572872 | tf_op jit(solution)/shard_map/ppermute | solution.py:30
  24.8 46.5 %all_gather.7 = bf16[32,64,128]{2,1,0:T(8,128)(2,1)S(1)} all-gather(bf16[2,64,128]{2,1,0:T(8,128)(2,1)S(1)} %fusion.12), channel_id=1, replica_groups=mesh['leaf'=16,'col'=2] {'leaf'}, dimensions={0}, use_global_device_ids=true | all-gather | bytes 557056 | tf_op jit(solution)/shard_map/all_gather | solution.py:86
  72.4 2.2 %collective-permute-start.5 = (bf16[2,64,128]{2,1,0:T(8,128)(2,1)S(1)}, bf16[2,64,128]{2,1,0:T(8,128)(2,1)S(1)}, u32[]{:S(2)}, u32[]{:S(2)}) collective-permute-start(bf16[2,64,128]{2,1,0:T(8,128)(2,1)S(1)} %collective-permute-done.4), channel_id=1, source_target_pairs={{0,2},{2,4},{4,6},{6,8},{8,10},{10,12},{12,14},{14,16},{16,18},{18... | collective-permute-start | bytes 98312 | tf_op jit(solution)/shard_map/ppermute | solution.py:16
  75.7 4.3 %collective-permute-done.5 = bf16[2,64,128]{2,1,0:T(8,128)(2,1)S(1)} collective-permute-done((bf16[2,64,128]{2,1,0:T(8,128)(2,1)S(1)}, bf16[2,64,128]{2,1,0:T(8,128)(2,1)S(1)}, u32[]{:S(2)}, u32[]{:S(2)}) %collective-permute-start.5) | collective-permute-done | bytes 32800 | tf_op jit(solution)/shard_map/ppermute | solution.py:16
  80.0 5.7 %collective-permute-start.13 = (bf16[2,64,128]{2,1,0:T(8,128)(2,1)S(1)}, bf16[2,64,128]{2,1,0:T(8,128)(2,1)S(1)}, u32[]{:S(2)}, u32[]{:S(2)}) collective-permute-start(bf16[2,64,128]{2,1,0:T(8,128)(2,1)S(1)} %collective-permute-done.12), channel_id=1, source_target_pairs={{0,30},{2,0},{4,2},{6,4},{8,6},{10,8},{12,10},{14,12},{16,14},{18,... | collective-permute-start | bytes 98312 | tf_op jit(solution)/shard_map/ppermute | solution.py:18
  85.7 1.8 %collective-permute-done.6 = bf16[2,64,128]{2,1,0:T(8,128)(2,1)S(1)} collective-permute-done((bf16[2,64,128]{2,1,0:T(8,128)(2,1)S(1)}, bf16[2,64,128]{2,1,0:T(8,128)(2,1)S(1)}, u32[]{:S(2)}, u32[]{:S(2)}) %collective-permute-start.6) | collective-permute-done | bytes 32800 | tf_op jit(solution)/shard_map/ppermute | solution.py:16
  87.5 5.7 %collective-permute-start.14 = (bf16[2,64,128]{2,1,0:T(8,128)(2,1)S(1)}, bf16[2,64,128]{2,1,0:T(8,128)(2,1)S(1)}, u32[]{:S(2)}, u32[]{:S(2)}) collective-permute-start(bf16[2,64,128]{2,1,0:T(8,128)(2,1)S(1)} %collective-permute-done.13), channel_id=1, source_target_pairs={{0,30},{2,0},{4,2},{6,4},{8,6},{10,8},{12,10},{14,12},{16,14},{18,... | collective-permute-start | bytes 98312 | tf_op jit(solution)/shard_map/ppermute | solution.py:18
  93.2 1.8 %collective-permute-done.7 = bf16[2,64,128]{2,1,0:T(8,128)(2,1)S(1)} collective-permute-done((bf16[2,64,128]{2,1,0:T(8,128)(2,1)S(1)}, bf16[2,64,128]{2,1,0:T(8,128)(2,1)S(1)}, u32[]{:S(2)}, u32[]{:S(2)}) %collective-permute-start.7) | collective-permute-done | bytes 32800 | tf_op jit(solution)/shard_map/ppermute | solution.py:16
  95.3 5.7 %collective-permute-start.15 = (bf16[2,64,128]{2,1,0:T(8,128)(2,1)S(1)}, bf16[2,64,128]{2,1,0:T(8,128)(2,1)S(1)}, u32[]{:S(2)}, u32[]{:S(2)}) collective-permute-start(bf16[2,64,128]{2,1,0:T(8,128)(2,1)S(1)} %collective-permute-done.14), channel_id=1, source_target_pairs={{0,30},{2,0},{4,2},{6,4},{8,6},{10,8},{12,10},{14,12},{16,14},{18,... | collective-permute-start | bytes 98312 | tf_op jit(solution)/shard_map/ppermute | solution.py:18
  101.0 1.6 collective-permute-done.8
  102.7 5.8 %collective-permute-start.16 = (bf16[2,64,128]{2,1,0:T(8,128)(2,1)S(1)}, bf16[2,64,128]{2,1,0:T(8,128)(2,1)S(1)}, u32[]{:S(2)}, u32[]{:S(2)}) collective-permute-start(bf16[2,64,128]{2,1,0:T(8,128)(2,1)S(1)} %collective-permute-done.15), channel_id=1, source_target_pairs={{0,30},{2,0},{4,2},{6,4},{8,6},{10,8},{12,10},{14,12},{16,14},{18,... | collective-permute-start | bytes 98312 | tf_op jit(solution)/shard_map/ppermute | solution.py:18
  108.5 1.7 collective-permute-done.9
  111.6 6.4 %collective-permute-start.17 = (bf16[2,64,128]{2,1,0:T(8,128)(2,1)S(1)}, bf16[2,64,128]{2,1,0:T(8,128)(2,1)S(1)}, u32[]{:S(2)}, u32[]{:S(2)}) collective-permute-start(bf16[2,64,128]{2,1,0:T(8,128)(2,1)S(1)} %collective-permute-done.16), channel_id=1, source_target_pairs={{0,30},{2,0},{4,2},{6,4},{8,6},{10,8},{12,10},{14,12},{16,14},{18,... | collective-permute-start | bytes 98312 | tf_op jit(solution)/shard_map/ppermute | solution.py:18
  118.8 3.1 %collective-permute-done.17 = bf16[2,64,128]{2,1,0:T(8,128)(2,1)S(1)} collective-permute-done((bf16[2,64,128]{2,1,0:T(8,128)(2,1)S(1)}, bf16[2,64,128]{2,1,0:T(8,128)(2,1)S(1)}, u32[]{:S(2)}, u32[]{:S(2)}) %collective-permute-start.17) | collective-permute-done | bytes 32800 | tf_op jit(solution)/shard_map/ppermute | solution.py:18
  121.9 3.6 %collective-permute-start.18 = (bf16[2,64,128]{2,1,0:T(8,128)(2,1)S(1)}, bf16[2,64,128]{2,1,0:T(8,128)(2,1)S(1)}, u32[]{:S(2)}, u32[]{:S(2)}) collective-permute-start(bf16[2,64,128]{2,1,0:T(8,128)(2,1)S(1)} %collective-permute-done.17), channel_id=1, source_target_pairs={{0,30},{2,0},{4,2},{6,4},{8,6},{10,8},{12,10},{14,12},{16,14},{18,... | collective-permute-start | bytes 98312 | tf_op jit(solution)/shard_map/ppermute | solution.py:18
  125.7 1.4 collective-permute-done.18
  129.3 1.9 %fusion.9 = f32[16,128,256]{2,1,0:T(8,128)} fusion(bf16[16,64,256]{2,1,0:T(8,128)(2,1)S(1)} %copy-done, f32[16,64,128]{2,1,0:T(8,128)S(1)} %bitcast.59, bf16[16,64,256]{2,1,0:T(8,128)(2,1)S(1)} %copy-done.3, bf16[16,256,128]{2,1,0:T(8,128)(2,1)S(1)} %bitcast.58), kind=kOutput, calls=%fused_computation.15 | convolution fusion | flops 134479872 | bytes 4718592 | tf_op jit(solution)/shard_map/lrk,lrc->lkc/dot_general | solution.py:118
  131.2 1.7 pad_maximum_fusion
  132.9 6.6 %gather_fusion = bf16[128,256,128]{2,1,0:T(8,128)(2,1)} fusion(bf16[32,256,128]{2,1,0:T(8,128)(2,1)S(1)} %bitcast.54, s32[1024]{0:T(1024)S(1)} %pad_clamp_fusion.2), kind=kCustom, calls=%fused_computation | custom fusion | bytes 16777728 | tf_op jit(solution)/shard_map/gather | solution.py:66
  139.5 12.1 %copy.26 = bf16[128,256,128]{1,2,0:T(8,128)(2,1)} copy(bf16[128,256,128]{2,1,0:T(8,128)(2,1)} %gather_fusion) | data formatting | bytes 16777216 | tf_op jit(solution)/shard_map/gather | solution.py:66
  151.6 12.7 %fusion.4 = f32[16,256,128]{1,2,0:T(8,128)} fusion(f32[16,128,256]{2,1,0:T(8,128)S(1)} %copy-done.2, bf16[16,8,256,256]{3,2,1,0:T(8,128)(2,1)} %all-gather.2.cloned.1.call-done, bf16[16,8,256,128]{2,3,1,0:T(8,128)(2,1)} %bitcast.56, pred[16,8]{1,0:T(8,128)(4,1)S(1)} %iota_compare_fusion), kind=kOutput, calls=%fused_computation.9 | convolution fusion | flops 2152202240 | bytes 29360256 | tf_op jit(solution)/shard_map/lsij,lsjc->lic/dot_general | solution.py:69
  164.3 2.9 %copy.34 = f32[16,256,128]{2,1,0:T(8,128)} copy(f32[16,256,128]{1,2,0:T(8,128)} %fusion.4) | data formatting | bytes 4194304 | tf_op jit(solution)/shard_map/add | solution.py:121
  (111 shorter events, 12.8 us)
Async XLA Ops:
  6.5 145.1 %all-gather.2.cloned.1.call-start = ((), (), s32[]{:S(2)}) async-start(), calls=%async_computation | async-start | bytes 25165824 | tf_op jit(solution)/shard_map/all_gather | solution.py:63
  7.3 72.7 %copy-start.7 = (s32[16,8]{0,1:T(8,128)S(1)}, s32[16,8]{0,1:T(8,128)}, u32[]{:S(2)}) copy-start(s32[16,8]{0,1:T(8,128)} %param.14) | copy-start | bytes 1540
  7.3 80.2 %copy-start.8 = (s32[16,4]{0,1:T(4,128)S(1)}, s32[16,4]{0,1:T(4,128)}, u32[]{:S(2)}) copy-start(s32[16,4]{0,1:T(4,128)} %param.18) | copy-start | bytes 772
  7.3 87.7 %copy-start.9 = (s32[16]{0:T(128)S(1)}, s32[16]{0:T(128)}, u32[]{:S(2)}) copy-start(s32[16]{0:T(128)} %param.15) | copy-start | bytes 196
  7.3 102.9 %copy-start.10 = (s32[2,4]{1,0:T(2,128)S(1)}, s32[2,4]{1,0:T(2,128)}, u32[]{:S(2)}) copy-start(s32[2,4]{1,0:T(2,128)} %param.21) | copy-start | bytes 100
  8.4 64.0 %collective-permute-start.4 = (bf16[2,64,128]{2,1,0:T(8,128)(2,1)S(1)}, bf16[2,64,128]{2,1,0:T(8,128)(2,1)S(1)}, u32[]{:S(2)}, u32[]{:S(2)}) collective-permute-start(bf16[2,64,128]{2,1,0:T(8,128)(2,1)S(1)} %bitcast.61), channel_id=1, source_target_pairs={{0,2},{2,4},{4,6},{6,8},{8,10},{10,12},{12,14},{14,16},{16,18},{18... | collective-permute-start | bytes 98312 | tf_op jit(solution)/shard_map/ppermute | solution.py:16
  11.5 68.6 %collective-permute-start.12 = (bf16[2,64,128]{2,1,0:T(8,128)(2,1)S(1)}, bf16[2,64,128]{2,1,0:T(8,128)(2,1)S(1)}, u32[]{:S(2)}, u32[]{:S(2)}) collective-permute-start(bf16[2,64,128]{2,1,0:T(8,128)(2,1)S(1)} %bitcast.62), channel_id=1, source_target_pairs={{0,30},{2,0},{4,2},{6,4},{8,6},{10,8},{12,10},{14,12},{16,14},{18,... | collective-permute-start | bytes 98312 | tf_op jit(solution)/shard_map/ppermute | solution.py:18
  15.5 94.7 %collective-permute-start.2 = (bf16[8,64,128]{2,1,0:T(8,128)(2,1)S(1)}, bf16[8,64,128]{2,1,0:T(8,128)(2,1)S(1)}, u32[]{:S(2)}, u32[]{:S(2)}) collective-permute-start(bf16[8,64,128]{2,1,0:T(8,128)(2,1)S(1)} %get-tuple-element.7), channel_id=1, source_target_pairs={{0,2},{2,4},{4,6},{6,8},{8,10},{10,12},{12,14},{14,16},{16,18},{18... | collective-permute-start | bytes 393224 | tf_op jit(solution)/shard_map/ppermute | solution.py:30
  16.8 101.1 %collective-permute-start.3 = (bf16[8,64,128]{2,1,0:T(8,128)(2,1)S(1)}, bf16[8,64,128]{2,1,0:T(8,128)(2,1)S(1)}, u32[]{:S(2)}, u32[]{:S(2)}) collective-permute-start(bf16[8,64,128]{2,1,0:T(8,128)(2,1)S(1)} %get-tuple-element.8), channel_id=1, source_target_pairs={{2,0},{4,2},{6,4},{8,6},{10,8},{12,10},{14,12},{16,14},{18,16},{20... | collective-permute-start | bytes 393224 | tf_op jit(solution)/shard_map/ppermute | solution.py:31
  19.2 112.0 %collective-permute-start = (bf16[2048,128]{1,0:T(8,128)(2,1)}, bf16[2048,128]{1,0:T(8,128)(2,1)}, u32[]{:S(2)}, u32[]{:S(2)}) collective-permute-start(bf16[2048,128]{1,0:T(8,128)(2,1)} %get-tuple-element.5), channel_id=1, source_target_pairs={{0,2},{2,4},{4,6},{6,8},{8,10},{10,12},{12,14},{14,16},{16,18},{18... | collective-permute-start | bytes 1572872 | tf_op jit(solution)/shard_map/ppermute | solution.py:30
  72.4 7.6 %collective-permute-start.5 = (bf16[2,64,128]{2,1,0:T(8,128)(2,1)S(1)}, bf16[2,64,128]{2,1,0:T(8,128)(2,1)S(1)}, u32[]{:S(2)}, u32[]{:S(2)}) collective-permute-start(bf16[2,64,128]{2,1,0:T(8,128)(2,1)S(1)} %collective-permute-done.4), channel_id=1, source_target_pairs={{0,2},{2,4},{4,6},{6,8},{8,10},{10,12},{12,14},{14,16},{16,18},{18... | collective-permute-start | bytes 98312 | tf_op jit(solution)/shard_map/ppermute | solution.py:16
  80.0 7.5 %collective-permute-start.6 = (bf16[2,64,128]{2,1,0:T(8,128)(2,1)S(1)}, bf16[2,64,128]{2,1,0:T(8,128)(2,1)S(1)}, u32[]{:S(2)}, u32[]{:S(2)}) collective-permute-start(bf16[2,64,128]{2,1,0:T(8,128)(2,1)S(1)} %collective-permute-done.5), channel_id=1, source_target_pairs={{0,2},{2,4},{4,6},{6,8},{8,10},{10,12},{12,14},{14,16},{16,18},{18... | collective-permute-start | bytes 98312 | tf_op jit(solution)/shard_map/ppermute | solution.py:16
  80.0 7.5 %collective-permute-start.13 = (bf16[2,64,128]{2,1,0:T(8,128)(2,1)S(1)}, bf16[2,64,128]{2,1,0:T(8,128)(2,1)S(1)}, u32[]{:S(2)}, u32[]{:S(2)}) collective-permute-start(bf16[2,64,128]{2,1,0:T(8,128)(2,1)S(1)} %collective-permute-done.12), channel_id=1, source_target_pairs={{0,30},{2,0},{4,2},{6,4},{8,6},{10,8},{12,10},{14,12},{16,14},{18,... | collective-permute-start | bytes 98312 | tf_op jit(solution)/shard_map/ppermute | solution.py:18
  87.5 7.5 %collective-permute-start.7 = (bf16[2,64,128]{2,1,0:T(8,128)(2,1)S(1)}, bf16[2,64,128]{2,1,0:T(8,128)(2,1)S(1)}, u32[]{:S(2)}, u32[]{:S(2)}) collective-permute-start(bf16[2,64,128]{2,1,0:T(8,128)(2,1)S(1)} %collective-permute-done.6), channel_id=1, source_target_pairs={{0,2},{2,4},{4,6},{6,8},{8,10},{10,12},{12,14},{14,16},{16,18},{18... | collective-permute-start | bytes 98312 | tf_op jit(solution)/shard_map/ppermute | solution.py:16
  87.5 7.8 %collective-permute-start.14 = (bf16[2,64,128]{2,1,0:T(8,128)(2,1)S(1)}, bf16[2,64,128]{2,1,0:T(8,128)(2,1)S(1)}, u32[]{:S(2)}, u32[]{:S(2)}) collective-permute-start(bf16[2,64,128]{2,1,0:T(8,128)(2,1)S(1)} %collective-permute-done.13), channel_id=1, source_target_pairs={{0,30},{2,0},{4,2},{6,4},{8,6},{10,8},{12,10},{14,12},{16,14},{18,... | collective-permute-start | bytes 98312 | tf_op jit(solution)/shard_map/ppermute | solution.py:18
  95.0 7.5 %collective-permute-start.8 = (bf16[2,64,128]{2,1,0:T(8,128)(2,1)S(1)}, bf16[2,64,128]{2,1,0:T(8,128)(2,1)S(1)}, u32[]{:S(2)}, u32[]{:S(2)}) collective-permute-start(bf16[2,64,128]{2,1,0:T(8,128)(2,1)S(1)} %collective-permute-done.7), channel_id=1, source_target_pairs={{0,2},{2,4},{4,6},{6,8},{8,10},{10,12},{12,14},{14,16},{16,18},{18... | collective-permute-start | bytes 98312 | tf_op jit(solution)/shard_map/ppermute | solution.py:16
  95.3 7.4 %collective-permute-start.15 = (bf16[2,64,128]{2,1,0:T(8,128)(2,1)S(1)}, bf16[2,64,128]{2,1,0:T(8,128)(2,1)S(1)}, u32[]{:S(2)}, u32[]{:S(2)}) collective-permute-start(bf16[2,64,128]{2,1,0:T(8,128)(2,1)S(1)} %collective-permute-done.14), channel_id=1, source_target_pairs={{0,30},{2,0},{4,2},{6,4},{8,6},{10,8},{12,10},{14,12},{16,14},{18,... | collective-permute-start | bytes 98312 | tf_op jit(solution)/shard_map/ppermute | solution.py:18
  102.5 7.6 %collective-permute-start.9 = (bf16[2,64,128]{2,1,0:T(8,128)(2,1)S(1)}, bf16[2,64,128]{2,1,0:T(8,128)(2,1)S(1)}, u32[]{:S(2)}, u32[]{:S(2)}) collective-permute-start(bf16[2,64,128]{2,1,0:T(8,128)(2,1)S(1)} %collective-permute-done.8), channel_id=1, source_target_pairs={{0,2},{2,4},{4,6},{6,8},{8,10},{10,12},{12,14},{14,16},{16,18},{18... | collective-permute-start | bytes 98312 | tf_op jit(solution)/shard_map/ppermute | solution.py:16
  102.7 8.8 %collective-permute-start.16 = (bf16[2,64,128]{2,1,0:T(8,128)(2,1)S(1)}, bf16[2,64,128]{2,1,0:T(8,128)(2,1)S(1)}, u32[]{:S(2)}, u32[]{:S(2)}) collective-permute-start(bf16[2,64,128]{2,1,0:T(8,128)(2,1)S(1)} %collective-permute-done.15), channel_id=1, source_target_pairs={{0,30},{2,0},{4,2},{6,4},{8,6},{10,8},{12,10},{14,12},{16,14},{18,... | collective-permute-start | bytes 98312 | tf_op jit(solution)/shard_map/ppermute | solution.py:18
  110.2 7.8 %collective-permute-start.10 = (bf16[2,64,128]{2,1,0:T(8,128)(2,1)S(1)}, bf16[2,64,128]{2,1,0:T(8,128)(2,1)S(1)}, u32[]{:S(2)}, u32[]{:S(2)}) collective-permute-start(bf16[2,64,128]{2,1,0:T(8,128)(2,1)S(1)} %collective-permute-done.9), channel_id=1, source_target_pairs={{0,2},{2,4},{4,6},{6,8},{8,10},{10,12},{12,14},{14,16},{16,18},{18... | collective-permute-start | bytes 98312 | tf_op jit(solution)/shard_map/ppermute | solution.py:16
  110.3 21.0 %collective-permute-start.1 = (bf16[2048,128]{1,0:T(8,128)(2,1)}, bf16[2048,128]{1,0:T(8,128)(2,1)}, u32[]{:S(2)}, u32[]{:S(2)}) collective-permute-start(bf16[2048,128]{1,0:T(8,128)(2,1)} %get-tuple-element.6), channel_id=1, source_target_pairs={{2,0},{4,2},{6,4},{8,6},{10,8},{12,10},{14,12},{16,14},{18,16},{20... | collective-permute-start | bytes 1572872 | tf_op jit(solution)/shard_map/ppermute | solution.py:31
  111.6 10.3 %collective-permute-start.17 = (bf16[2,64,128]{2,1,0:T(8,128)(2,1)S(1)}, bf16[2,64,128]{2,1,0:T(8,128)(2,1)S(1)}, u32[]{:S(2)}, u32[]{:S(2)}) collective-permute-start(bf16[2,64,128]{2,1,0:T(8,128)(2,1)S(1)} %collective-permute-done.16), channel_id=1, source_target_pairs={{0,30},{2,0},{4,2},{6,4},{8,6},{10,8},{12,10},{14,12},{16,14},{18,... | collective-permute-start | bytes 98312 | tf_op jit(solution)/shard_map/ppermute | solution.py:18
  118.0 7.5 %collective-permute-start.11 = (bf16[2,64,128]{2,1,0:T(8,128)(2,1)S(1)}, bf16[2,64,128]{2,1,0:T(8,128)(2,1)S(1)}, u32[]{:S(2)}, u32[]{:S(2)}) collective-permute-start(bf16[2,64,128]{2,1,0:T(8,128)(2,1)S(1)} %collective-permute-done.10), channel_id=1, source_target_pairs={{0,2},{2,4},{4,6},{6,8},{8,10},{10,12},{12,14},{14,16},{16,18},{18... | collective-permute-start | bytes 98312 | tf_op jit(solution)/shard_map/ppermute | solution.py:16
  121.9 5.2 %collective-permute-start.18 = (bf16[2,64,128]{2,1,0:T(8,128)(2,1)S(1)}, bf16[2,64,128]{2,1,0:T(8,128)(2,1)S(1)}, u32[]{:S(2)}, u32[]{:S(2)}) collective-permute-start(bf16[2,64,128]{2,1,0:T(8,128)(2,1)S(1)} %collective-permute-done.17), channel_id=1, source_target_pairs={{0,30},{2,0},{4,2},{6,4},{8,6},{10,8},{12,10},{14,12},{16,14},{18,... | collective-permute-start | bytes 98312 | tf_op jit(solution)/shard_map/ppermute | solution.py:18
  (7 other events, 109.5 us)
Sparse Core Ops, SparseCore 0:
  8.9 32.7 all-gather.1
